TPU v7x, 1024 devices: a whole 4x4x32 slice. The times are simulated.
1024 devices in a mesh: seq: 128 (over x_lo, z, core), chan: 8 (over y, x_hi).
Axes of the slice: x: 4 (x_hi: 2, x_lo: 2; x = x_hi * 2 + x_lo), y: 4, z: 32, core: 2. Of those that a mesh axis runs over, the one named last changes fastest.
Arguments:
- grad_out: bfloat16 [16384, 4096], P('seq', 'chan'), may hold values from -6 to 6
- out_weight: bfloat16 [4096, 4096], P('seq', 'chan'), may hold values from -0.09375 to 0.09375
- gate_stream: bfloat16 [4096, 16384], P('chan', 'seq'), may hold values from -6 to 6
- conv_output: bfloat16 [4096, 16384], P('chan', 'seq'), may hold values from -6 to 6
- key_stream: bfloat16 [4096, 16384], P('chan', 'seq'), may hold values from -6 to 6
- value_stream: bfloat16 [4096, 16384], P('chan', 'seq'), may hold values from -6 to 6
- long_filter: bfloat16 [4096, 16384], P(('chan', 'seq')), may hold values from 0 to 1
Outputs:
- grad_gate: bfloat16 [4096, 16384], P('chan', 'seq')
- grad_key: bfloat16 [4096, 16384], P('chan', 'seq')
- grad_value: bfloat16 [4096, 16384], P('chan', 'seq')
All inputs are finite; a program needn't handle non-finite values.
Results may differ from a plain program's by a relative error of at most 0.007.
Values may be sent and summed in bfloat16 or wider, within the bound.
A program may use at most 64 MiB of HBM per device.

v0:
```python
import math

import jax
import jax.numpy as jnp
from jax import lax
from jax.sharding import PartitionSpec as P


def dft_tables(count_outer, count_inner):
    total_len = count_outer * count_inner
    index_outer = jnp.arange(count_outer, dtype=jnp.int32)
    index_inner = jnp.arange(count_inner, dtype=jnp.int32)
    angle_outer = (index_outer[:, None] * index_outer[None, :] % count_outer).astype(
        jnp.float32
    ) * (2.0 * math.pi / count_outer)
    angle_inner = (index_inner[:, None] * index_inner[None, :] % count_inner).astype(
        jnp.float32
    ) * (2.0 * math.pi / count_inner)
    angle_twist = (index_outer[:, None] * index_inner[None, :] % total_len).astype(jnp.float32) * (
        2.0 * math.pi / total_len
    )
    return (
        jnp.cos(angle_outer),
        -jnp.sin(angle_outer),
        jnp.cos(angle_inner),
        -jnp.sin(angle_inner),
        jnp.cos(angle_twist),
        -jnp.sin(angle_twist),
    )


def outer_exact(table, signal):
    table_high = table.astype(jnp.bfloat16)
    table_low = (table - table_high.astype(jnp.float32)).astype(jnp.bfloat16)
    first = jnp.einsum("ab,cbk->cak", table_high, signal, preferred_element_type=jnp.float32)
    return first + jnp.einsum("ab,cbk->cak", table_low, signal, preferred_element_type=jnp.float32)


def outer_wide(table, values):
    return jnp.einsum(
        "ab,cbk->cak",
        table,
        values,
        precision=lax.Precision.HIGH,
        preferred_element_type=jnp.float32,
    )


def inner_wide(values, table):
    return jnp.einsum(
        "cak,kl->cal",
        values,
        table,
        precision=lax.Precision.HIGH,
        preferred_element_type=jnp.float32,
    )


def spectral_forward(signal, tables):
    outer_cos, outer_sin, inner_cos, inner_sin, twist_cos, twist_sin = tables
    part_re = outer_exact(outer_cos, signal)
    part_im = outer_exact(outer_sin, signal)
    turned_re = part_re * twist_cos - part_im * twist_sin
    turned_im = part_re * twist_sin + part_im * twist_cos
    spec_re = inner_wide(turned_re, inner_cos) - inner_wide(turned_im, inner_sin)
    spec_im = inner_wide(turned_re, inner_sin) + inner_wide(turned_im, inner_cos)
    return (spec_re, spec_im)


def spectral_inverse_real(spec_re, spec_im, tables):
    outer_cos, outer_sin, inner_cos, inner_sin, twist_cos, twist_sin = tables
    back_re = inner_wide(spec_re, inner_cos) + inner_wide(spec_im, inner_sin)
    back_im = inner_wide(spec_im, inner_cos) - inner_wide(spec_re, inner_sin)
    turned_re = back_re * twist_cos + back_im * twist_sin
    turned_im = back_im * twist_cos - back_re * twist_sin
    total_len = spec_re.shape[1] * spec_re.shape[2]
    return (outer_wide(outer_cos, turned_re) + outer_wide(outer_sin, turned_im)) / total_len


def correlate(gathered, filters, tables):
    channel_count, seq_len = gathered.shape
    count_outer = tables[0].shape[0]
    count_inner = tables[2].shape[0]
    padding = jnp.zeros((2 * channel_count, seq_len), jnp.bfloat16)
    stacked = jnp.concatenate([gathered, filters], axis=0)
    padded = jnp.concatenate([stacked, padding], axis=1).reshape(
        2 * channel_count, count_outer, count_inner
    )
    both_re, both_im = spectral_forward(padded, tables)
    signal_re, kernel_re = (both_re[:channel_count], both_re[channel_count:])
    signal_im, kernel_im = (both_im[:channel_count], both_im[channel_count:])
    joined_re = kernel_re * signal_re + kernel_im * signal_im
    joined_im = kernel_re * signal_im - kernel_im * signal_re
    result = spectral_inverse_real(joined_re, joined_im, tables)
    return result.reshape(channel_count, -1)[:, :seq_len].astype(jnp.bfloat16)


def per_device(
    grad_out, out_weight, gate_stream, conv_output, key_stream, value_stream, long_filter
):
    seq_count = lax.axis_size("seq")
    token_count = grad_out.shape[0]
    chan_width = out_weight.shape[1]
    group_width = chan_width // seq_count
    full_grad = lax.all_gather(grad_out, "chan", axis=1, tiled=True)
    tables = dft_tables(2 * seq_count, token_count)
    grad_mix = jnp.einsum(
        "nc,tn->ct",
        lax.all_gather(out_weight, "seq", axis=0, tiled=True),
        full_grad,
        preferred_element_type=jnp.float32,
    )
    gated_grad = (grad_mix * gate_stream.astype(jnp.float32)).astype(jnp.bfloat16)
    regrouped = lax.all_to_all(
        gated_grad.reshape(seq_count, group_width, token_count),
        "seq",
        split_axis=0,
        concat_axis=2,
        tiled=True,
    )
    inner_grad = correlate(regrouped[0], long_filter, tables)
    returned = lax.all_to_all(inner_grad[None], "seq", split_axis=2, concat_axis=0, tiled=True)
    grad_inner = returned.reshape(chan_width, token_count)
    grad_gate = (grad_mix * conv_output.astype(jnp.float32)).astype(jnp.bfloat16)
    inner_grad_wide = grad_inner.astype(jnp.float32)
    grad_key = (inner_grad_wide * value_stream.astype(jnp.float32)).astype(jnp.bfloat16)
    grad_value = (inner_grad_wide * key_stream.astype(jnp.float32)).astype(jnp.bfloat16)
    return (grad_gate, grad_key, grad_value)


def solution(mesh):
    in_specs = (
        P("seq", "chan"),
        P("seq", "chan"),
        P("chan", "seq"),
        P("chan", "seq"),
        P("chan", "seq"),
        P("chan", "seq"),
        P(("chan", "seq"), None),
    )
    out_specs = (P("chan", "seq"), P("chan", "seq"), P("chan", "seq"))
    return jax.shard_map(
        per_device, mesh=mesh, in_specs=in_specs, out_specs=out_specs, check_vma=False
    )
```

profile of v0, /device:TPU:1, one launch (start us, length us, event | category | flops | bytes accessed | tf_op | source)
XLA Modules:
  0.0 595.3 jit_solution(14957696650811767647)
XLA Ops:
  7.2 0.0 all-gather.5.cloned.1.call-start
  7.2 0.7 all-gather.5.cloned.1.call-update
  7.9 0.0 all-gather.3.cloned.1.call-start
  7.9 0.7 all-gather.3.cloned.1.call-update
  8.6 91.9 %all-gather.5.cloned.1.call-done = bf16[128,4096]{1,0:T(8,128)(2,1)} async-done(((bf16[128,512]{1,0:T(8,128)(2,1)}), bf16[128,4096]{1,0:T(8,128)(2,1)}) %all-gather.5.cloned.1.call-update) | async-done | bytes 1048592 | tf_op jit(solution)/shard_map/all_gather | solution.py:105
  100.5 240.5 %all-gather.3.cloned.1.call-done = bf16[4096,512]{1,0:T(8,128)(2,1)} async-done(((bf16[32,512]{1,0:T(8,128)(2,1)}), bf16[4096,512]{1,0:T(8,128)(2,1)}) %all-gather.3.cloned.1.call-update) | async-done | bytes 4194320 | tf_op jit(solution)/shard_map/all_gather | solution.py:109
  341.0 4.5 multiply_convert_fusion.2
  345.6 16.3 %all-to-all-start = ((bf16[128,4,128]{2,1,0:T(4,128)(2,1)}), bf16[128,4,128]{2,1,0:T(4,128)(2,1)S(1)}, u32[]{:S(2)}, u32[]{:S(2)}) async-start(bf16[128,4,128]{2,1,0:T(4,128)(2,1)} %bitcast), calls=%async_computation | async-start | bytes 262144 | tf_op jit(solution)/shard_map/all_to_all | solution.py:114
  361.8 0.5 sine_negate_fusion.2
  362.4 0.1 copy.44
  362.5 0.1 copy.43
  362.6 24.9 %all-to-all-done = bf16[128,4,128]{2,1,0:T(4,128)(2,1)S(1)} async-done(((bf16[128,4,128]{2,1,0:T(4,128)(2,1)}), bf16[128,4,128]{2,1,0:T(4,128)(2,1)S(1)}, u32[]{:S(2)}, u32[]{:S(2)}) %all-to-all-start) | async-done | bytes 131104 | tf_op jit(solution)/shard_map/all_to_all | solution.py:114
  387.5 1.1 fusion.8
  388.5 1.3 fusion.10
  389.8 1.3 fusion.13
  391.1 1.3 fusion
  392.4 1.3 fusion.1
  393.6 1.2 fusion.38
  394.9 1.2 fusion.39
  396.1 1.2 convolution_add_fusion
  397.3 1.2 convolution_subtract_fusion
  398.5 0.1 multiply_add_fusion.1
  398.6 0.6 fusion.72
  399.2 0.8 fusion.70
  400.1 0.6 convolution_add_fusion.3
  400.7 0.6 convolution_subtract_fusion.1
  401.3 1.5 fusion.18
  402.8 1.5 fusion.4
  404.3 0.2 copy.47
  404.5 0.2 copy.79
  404.8 12.9 %copy.48 = bf16[1,4,16384]{1,0,2:T(2,128)(2,1)} copy(bf16[1,4,16384]{2,1,0:T(4,128)(2,1)S(1)} %slice_bitcast_fusion) | data formatting | bytes 262144 | tf_op jit(solution)/shard_map/broadcast_in_dim | solution.py:122
  417.6 0.5 broadcast.140
  418.2 90.8 %reduce = bf16[16384,4]{1,0:T(8,128)(2,1)} reduce(bf16[16384,1,4]{2,1,0:T(2,128)(2,1)} %bitcast.78, bf16[]{:T(256)} %broadcast.140), dimensions={1}, to_apply=%bitcast.68.reduce_sub_computation | reduce | bytes 262146
  508.9 8.7 %reshape.73 = bf16[128,2,256]{2,1,0:T(2,128)(2,1)S(1)} reshape(bf16[16384,4]{1,0:T(8,128)(2,1)} %reduce) | data formatting | bytes 262144
  517.6 36.6 %all_to_all.24 = bf16[128,2,256]{2,1,0:T(2,128)(2,1)S(1)} all-to-all(bf16[128,2,256]{2,1,0:T(2,128)(2,1)S(1)} %reshape.73), channel_id=1, replica_groups=mesh['seq'=128,'chan'=8] {'seq'}, dimensions={0} | all-to-all | bytes 262144 | tf_op jit(solution)/shard_map/all_to_all | solution.py:122
  554.2 17.1 %reshape.74 = bf16[16384,1,4]{2,1,0:T(2,128)(2,1)} reshape(bf16[128,2,256]{2,1,0:T(2,128)(2,1)S(1)} %all_to_all.24) | data formatting | bytes 262144
  571.3 10.8 %bitcast_convert_fusion = f32[1,4,16384]{1,0,2:T(1,128)} fusion(bf16[16384,1,4]{2,1,0:T(2,128)(2,1)} %reshape.74), kind=kLoop, calls=%fused_computation.159 | loop fusion | flops 65536 | bytes 393216 | tf_op jit(solution)/shard_map/convert_element_type | solution.py:125
  582.1 0.0 copy-start
  582.1 0.0 copy-start.1
  582.1 5.5 copy.49
  587.6 0.0 copy-done
  587.7 0.0 copy-done.1
  587.7 0.8 multiply_convert_fusion
  (1 shorter events, 0.0 us)
Async XLA Ops:
  7.2 93.4 %all-gather.5.cloned.1.call-start = ((), (), s32[]{:S(2)}) async-start(), calls=%async_computation.3 | async-start | bytes 1179648 | tf_op jit(solution)/shard_map/all_gather | solution.py:105
  7.9 333.1 %all-gather.3.cloned.1.call-start = ((), (), s32[]{:S(2)}) async-start(), calls=%async_computation.2 | async-start | bytes 4227072 | tf_op jit(solution)/shard_map/all_gather | solution.py:109
  345.6 41.9 %all-to-all-start = ((bf16[128,4,128]{2,1,0:T(4,128)(2,1)}), bf16[128,4,128]{2,1,0:T(4,128)(2,1)S(1)}, u32[]{:S(2)}, u32[]{:S(2)}) async-start(bf16[128,4,128]{2,1,0:T(4,128)(2,1)} %bitcast), calls=%async_computation | async-start | bytes 262144 | tf_op jit(solution)/shard_map/all_to_all | solution.py:114
  582.1 5.6 copy-start
  582.1 5.6 copy-start.1
Sparse Core Ops, SparseCore 0:
  12.2 88.2 all-gather.4
  103.3 237.7 all-gather.2
where the time goes:
time: 596 us; the launch traced here: 595 us
  waiting for transfers between devices  359 us (60%)
  other arithmetic  104 us (17%)
  local copies, waits for them, and re-layouts  45.3 us (8%)
  blocking collectives  36.6 us (6%)
  matrix products  20.1 us (3%)
  starting transfers between devices  16.3 us (3%)
  between operations  14.2 us (2%)
    all_gather x1, waiting for transfers between devices, per_device(): lax.all_gather(out_weight, 'seq', axis=0, tiled=True)  241 us
    all_gather x1, waiting for transfers between devices, per_device(): full_grad = lax.all_gather(grad_out, 'chan', axis=1, tiled=True)  91.9 us
    unnamed x2, other arithmetic  91.8 us
    all_to_all x1, blocking collectives, per_device(): lax.all_to_all(inner_grad[None], 'seq', split_axis=2, concat_axis=0, tile...  36.6 us
    unnamed x8, local copies, waits for them, and re-layouts  26.5 us
    all_to_all x1, waiting for transfers between devices, per_device(): lax.all_to_all(gated_grad.reshape(seq_count, group_width, token_count), '...  24.9 us
    all_to_all x1, starting transfers between devices, per_device(): lax.all_to_all(gated_grad.reshape(seq_count, group_width, token_count), '...  16.3 us
    broadcast_in_dim x2, local copies, waits for them, and re-layouts, per_device(): inner_grad[None]  12.9 us
  transfers between devices with their start and end apart: 3, of which 3 were waited for; matrix products, arithmetic and copies ran while one was open for 0% of the time, Pallas kernels for 0%

commit v1 on v0

v1 whole, which is shorter than its diff:
```python
import functools
import math

import jax
import jax.numpy as jnp
import numpy as np
from jax import lax
from jax.experimental import pallas as pl
from jax.experimental.pallas import tpu as pltpu
from jax.sharding import PartitionSpec as P

MESH = pl.DeviceIdType.MESH
ZN = 32
CHAN = 8
VMEM = pltpu.VMEM


def seq_index(x, z, core):
    return (x * ZN + z) * 2 + core


def my_place():
    me = lax.axis_index("seq")
    return me, me // (2 * ZN), lax.rem(me // 2, ZN), lax.rem(me, 2)


def gather_kernel(g_ref, w_ref, gate_ref, conv_ref, gg_ref, gated_ref, wf, gf, acc,
                  recv_r, recv_l, recv_x, recv_p, recv_q, recv_g, send_w, send_q, send_g, local):
    me, x, z, core = my_place()
    chan = lax.axis_index("chan")
    zr, zl = lax.rem(z + 1, ZN), lax.rem(z + ZN - 1, ZN)
    right, left = seq_index(x, zr, core), seq_index(x, zl, core)
    partner, across = seq_index(x, z, 1 - core), seq_index(1 - x, z, core)

    barrier = pltpu.get_barrier_semaphore()
    for peer in (right, left, partner, across):
        pl.semaphore_signal(barrier, inc=1, device_id={"seq": peer}, device_id_type=MESH)
    for step in range(1, CHAN):
        pl.semaphore_signal(barrier, inc=1, device_id={"chan": lax.rem(chan + step, CHAN)}, device_id_type=MESH)
    own_w = pltpu.make_async_copy(w_ref, wf.at[x, z, core], local.at[0])
    own_w.start()
    own_g = pltpu.make_async_copy(g_ref, gf.at[chan], local.at[1])
    own_g.start()
    pl.semaphore_wait(barrier, 4 + CHAN - 1)

    def send(src, slot_z, target, send_sem, recv_sem):
        pltpu.make_async_remote_copy(
            src_ref=src, dst_ref=wf.at[x, slot_z, core], send_sem=send_sem, recv_sem=recv_sem,
            device_id={"seq": target}, device_id_type=MESH,
        ).start()

    send(w_ref, z, right, send_w, recv_r.at[0])
    send(w_ref, z, left, send_w, recv_l.at[0])
    send(w_ref, z, across, send_w, recv_x)
    send(w_ref, z, partner, send_w, recv_p)
    for step in range(1, CHAN):
        pltpu.make_async_remote_copy(
            src_ref=g_ref, dst_ref=gf.at[chan], send_sem=send_g, recv_sem=recv_g,
            device_id={"chan": lax.rem(chan + step, CHAN)}, device_id_type=MESH,
        ).start()

    def arrived(slot_z, sem):
        here = wf.at[x, slot_z, core]
        pltpu.make_async_copy(here, here, sem).wait()
        return here

    def hop(k, _):
        from_left, from_right = lax.rem(z + 2 * ZN - 1 - k, ZN), lax.rem(z + 1 + k, ZN)
        shard = arrived(from_left, recv_r.at[k])
        send(shard, from_left, right, send_w, recv_r.at[k + 1])
        other = arrived(from_right, recv_l.at[k])

        @pl.when(k < 14)
        def _():
            send(other, from_right, left, send_w, recv_l.at[k + 1])

        send(shard, from_left, across, send_w, recv_x)
        send(other, from_right, across, send_w, recv_x)
        send(shard, from_left, partner, send_w, recv_p)
        send(other, from_right, partner, send_w, recv_p)
        return 0

    lax.fori_loop(0, 15, hop, 0)
    last = lax.rem(z + 16, ZN)
    shard = arrived(last, recv_r.at[15])
    send(shard, last, across, send_w, recv_x)
    send(shard, last, partner, send_w, recv_p)

    quarter = wf.at[1 - x, :, core]
    pltpu.make_async_copy(quarter, quarter, recv_x).wait()
    pltpu.make_async_remote_copy(
        src_ref=quarter, dst_ref=quarter, send_sem=send_q, recv_sem=recv_q,
        device_id={"seq": partner}, device_id_type=MESH,
    ).start()

    own_w.wait()
    own_g.wait()
    others = gf.at[pl.ds(0, CHAN - 1)]
    pltpu.make_async_copy(others, others, recv_g).wait()
    theirs = wf.at[x, :, 1 - core]
    pltpu.make_async_copy(theirs, theirs, recv_p).wait()
    diagonal = wf.at[1 - x, :, 1 - core]
    pltpu.make_async_copy(diagonal, diagonal, recv_q).wait()

    acc[...] = jnp.zeros_like(acc)

    def multiply(j, _):
        block = wf[j // 4, pl.ds(lax.rem(j, 4) * 8, 8)].reshape(512, 512)
        acc[...] += jnp.dot(gf[j], block, preferred_element_type=jnp.float32)
        return 0

    lax.fori_loop(0, CHAN, multiply, 0)
    mix = acc[...].T
    gg_ref[...] = (mix * conv_ref[...].astype(jnp.float32)).astype(jnp.bfloat16)
    gated_ref[...] = (mix * gate_ref[...].astype(jnp.float32)).astype(jnp.bfloat16)

    pltpu.make_async_copy(quarter, quarter, send_q).wait()
    pltpu.make_async_copy(others, others, send_g).wait()
    for amount in (quarter, quarter):
        pltpu.make_async_copy(amount, amount, send_w).wait()
    rest = wf.at[x, pl.ds(0, 31), core]
    pltpu.make_async_copy(rest, rest, send_w).wait()


def gather_multiply(grad_out, out_weight, gate_stream, conv_output):
    space = pl.BlockSpec(memory_space=VMEM)
    dma = pltpu.SemaphoreType.DMA
    out = jax.ShapeDtypeStruct((512, 128), jnp.bfloat16)
    return pl.pallas_call(
        gather_kernel,
        out_shape=(out, out),
        in_specs=[space] * 4,
        out_specs=(space, space),
        scratch_shapes=[
            VMEM((2, ZN, 2, 32, 512), jnp.bfloat16),
            VMEM((CHAN, 128, 512), jnp.bfloat16),
            VMEM((128, 512), jnp.float32),
            dma((16,)), dma((16,)), dma, dma, dma, dma, dma, dma, dma, dma((2,)),
        ],
        compiler_params=pltpu.CompilerParams(collective_id=0, has_side_effects=True, vmem_limit_bytes=32 << 20),
        name="gather_multiply",
    )(grad_out, out_weight, gate_stream, conv_output)


def exchange_kernel(x_ref, o_ref, barrier_unused, recv, sent, local):
    me, x, z, core = my_place()

    def peers(act):
        def body(m, _):
            k = (m + 1) // 2
            away = 16 - k
            there = lax.rem(z + ZN + away * (2 * lax.rem(m, 2) - 1), ZN)
            for flip_x, flip_core in ((1, 0), (1, 1), (0, 0), (0, 1)):
                other_x = x + flip_x * (1 - 2 * x)
                other_core = core + flip_core * (1 - 2 * core)
                if flip_x == 0 and flip_core == 0:
                    @pl.when(m < ZN - 1)
                    def _():
                        act(seq_index(other_x, there, other_core))
                else:
                    act(seq_index(other_x, there, other_core))
            return 0

        lax.fori_loop(0, ZN, body, 0)

    barrier = pltpu.get_barrier_semaphore()
    peers(lambda peer: pl.semaphore_signal(barrier, inc=1, device_id={"seq": peer}, device_id_type=MESH))
    own = pltpu.make_async_copy(x_ref.at[me], o_ref.at[me], local)
    own.start()
    pl.semaphore_wait(barrier, 127)
    peers(lambda peer: pltpu.make_async_remote_copy(
        src_ref=x_ref.at[peer], dst_ref=o_ref.at[me], send_sem=sent, recv_sem=recv,
        device_id={"seq": peer}, device_id_type=MESH).start())
    own.wait()
    most = o_ref.at[pl.ds(0, 127)]
    pltpu.make_async_copy(most, most, recv).wait()
    pltpu.make_async_copy(most, most, sent).wait()


def exchange(blocks):
    space = pl.BlockSpec(memory_space=VMEM)
    dma = pltpu.SemaphoreType.DMA
    return pl.pallas_call(
        exchange_kernel,
        out_shape=jax.ShapeDtypeStruct(blocks.shape, blocks.dtype),
        in_specs=[space],
        out_specs=space,
        scratch_shapes=[pltpu.SemaphoreType.REGULAR, dma, dma, dma],
        compiler_params=pltpu.CompilerParams(collective_id=1, has_side_effects=True),
        name="exchange",
    )(blocks)


def tables(outer, inner):
    total = outer * inner
    def angles(a, b, n):
        return 2.0 * np.pi * ((np.arange(a)[:, None] * np.arange(b)[None, :]) % n) / n
    out = angles(outer, outer, outer)
    inn = angles(inner, inner, inner)
    twist = angles(outer, inner, total)
    f = np.float32
    return tuple(v.astype(f) for v in (np.cos(out), -np.sin(out), np.cos(inn), -np.sin(inn), np.cos(twist), -np.sin(twist)))


def outer_exact(table, signal):
    high = jnp.asarray(table).astype(jnp.bfloat16)
    low = (jnp.asarray(table) - high.astype(jnp.float32)).astype(jnp.bfloat16)
    first = jnp.einsum("ab,cbk->cak", high, signal, preferred_element_type=jnp.float32)
    return first + jnp.einsum("ab,cbk->cak", low, signal, preferred_element_type=jnp.float32)


def wide(spec, a, b):
    return jnp.einsum(spec, a, b, precision=lax.Precision.HIGH, preferred_element_type=jnp.float32)


def correlate(blocks, filters):
    channels = blocks.shape[1]
    oc, os_, ic, is_, tc, ts = tables(256, 128)
    both = jnp.concatenate([jnp.swapaxes(blocks, 0, 1), filters], axis=0)
    p_re = outer_exact(oc[:, :128], both)
    p_im = outer_exact(os_[:, :128], both)
    t_re = p_re * tc - p_im * ts
    t_im = p_re * ts + p_im * tc
    inner = "cak,kl->cal"
    s_re = wide(inner, t_re, ic) - wide(inner, t_im, is_)
    s_im = wide(inner, t_re, is_) + wide(inner, t_im, ic)
    a_re, k_re = s_re[:channels], s_re[channels:]
    a_im, k_im = s_im[:channels], s_im[channels:]
    j_re = k_re * a_re + k_im * a_im
    j_im = k_re * a_im - k_im * a_re
    b_re = wide(inner, j_re, ic) + wide(inner, j_im, is_)
    b_im = wide(inner, j_im, ic) - wide(inner, j_re, is_)
    v_re = b_re * tc + b_im * ts
    v_im = b_im * tc - b_re * ts
    outer = "ab,cbk->cak"
    full = (wide(outer, oc[:128], v_re) + wide(outer, os_[:128], v_im)) / (256 * 128)
    return jnp.swapaxes(full.astype(jnp.bfloat16), 0, 1)


def per_device(grad_out, out_weight, gate_stream, conv_output, key_stream, value_stream, long_filter):
    grad_gate, gated = gather_multiply(grad_out, out_weight, gate_stream, conv_output)
    blocks = exchange(gated.reshape(128, 4, 128))
    inner = correlate(blocks, long_filter.reshape(4, 128, 128))
    grad_inner = exchange(inner).reshape(512, 128).astype(jnp.float32)
    grad_key = (grad_inner * value_stream.astype(jnp.float32)).astype(jnp.bfloat16)
    grad_value = (grad_inner * key_stream.astype(jnp.float32)).astype(jnp.bfloat16)
    return (grad_gate, grad_key, grad_value)


def solution(mesh):
    in_specs = (
        P("seq", "chan"), P("seq", "chan"), P("chan", "seq"), P("chan", "seq"),
        P("chan", "seq"), P("chan", "seq"), P(("chan", "seq"), None),
    )
    out_specs = (P("chan", "seq"), P("chan", "seq"), P("chan", "seq"))
    return jax.shard_map(per_device, mesh=mesh, in_specs=in_specs, out_specs=out_specs, check_vma=False)
```

time: 596 us -> 162 us (0.27)
  waiting for transfers between devices: 359 us -> 0 us
  Pallas kernels: 0 us -> 140 us
  other arithmetic: 104 us -> 2.83 us
  blocking collectives: 36.6 us -> 0 us
  local copies, waits for them, and re-layouts: 45.3 us -> 9.63 us
  starting transfers between devices: 16.3 us -> 0 us
  between operations: 14.2 us -> 0.86 us
  matrix products: 20.1 us -> 7.84 us
    all_gather x2 -> x0, waiting for transfers between devices: 332 us -> none  [the longest x1 241 us: per_device(): lax.all_gather(out_weight, 'seq', axis=0, tiled=True)]
    pallas_call x0 -> x3, Pallas kernels: none -> 140 us  [the longest x1 81.7 us: gather_multiply(): pl.pallas_call(gather_kernel, out_shape=(out, out), in_specs=[space] * 4,...]
    unnamed x2 -> x0, other arithmetic: 91.8 us -> none
    all_to_all x1 -> x0, blocking collectives: 36.6 us -> none  [per_device(): lax.all_to_all(inner_grad[None], 'seq', split_axis=2, concat_axis=0, tile...]
    all_to_all x1 -> x0, waiting for transfers between devices: 24.9 us -> none  [per_device(): lax.all_to_all(gated_grad.reshape(seq_count, group_width, token_count), '...]
    unnamed x8 -> x42, local copies, waits for them, and re-layouts: 26.5 us -> 9.41 us
    all_to_all x1 -> x0, starting transfers between devices: 16.3 us -> none  [per_device(): lax.all_to_all(gated_grad.reshape(seq_count, group_width, token_count), '...]
    broadcast_in_dim x2 -> x0, local copies, waits for them, and re-layouts: 12.9 us -> none  [per_device(): inner_grad[None]]
  transfers between devices with their start and end apart: 3 -> 0, of which waited for: 3 -> 0; matrix products, arithmetic and copies ran while one was open for 0% -> 0% of each run, Pallas kernels for 0% -> 0%
where the time goes in v1:
time: 162 us; the launch traced here: 161 us
  Pallas kernels  140 us (86%)
  local copies, waits for them, and re-layouts  9.63 us (6%)
  matrix products  7.84 us (5%)
  other arithmetic  2.83 us (2%)
    pallas_call x1, Pallas kernels, gather_multiply(): pl.pallas_call(gather_kernel, out_shape=(out, out), in_specs=[space] * 4,...  81.7 us
    pallas_call x2, Pallas kernels, exchange(): pl.pallas_call(exchange_kernel, out_shape=jax.ShapeDtypeStruct(blocks.sha...  58.4 us
    unnamed x42, local copies, waits for them, and re-layouts  9.41 us
    dot_general x10, matrix products, wide(): jnp.einsum(spec, a, b, precision=lax.Precision.HIGH, preferred_element_ty...  6.69 us

profile of v1, /device:TPU:1, one launch (start us, length us, event | category | flops | bytes accessed | tf_op | source)
XLA Modules:
  0.0 161.2 jit_solution(45842878393184047)
XLA Ops:
  0.6 0.0 copy-start
  0.6 0.9 copy-done
  1.5 0.0 copy-start.1
  1.5 0.9 copy-done.1
  2.4 0.0 copy-start.2
  2.4 0.9 copy-done.2
  3.3 0.0 copy-start.4
  3.3 0.8 copy-done.4
  4.1 81.7 %gather_multiply.1 = (bf16[512,128]{1,0:T(8,128)(2,1)S(1)}, bf16[512,128]{1,0:T(8,128)(2,1)S(1)}) custom-call(bf16[128,512]{1,0:T(8,128)(2,1)S(1)} %copy-done, bf16[32,512]{1,0:T(8,128)(2,1)S(1)} %copy-done.4, bf16[512,128]{1,0:T(8,128)(2,1)S(1)} %copy-done.1, bf16[512,128]{1,0:T(8,128)(2,1)S(1)} %copy-done.2), custom_call_target="tpu_custom_call" | custom-call | tf_op jit(solution)/shard_map/gather_multiply/pallas_call | solution.py:129
  85.8 0.0 copy-start.3
  85.8 0.6 copy-done.3
  86.5 0.0 copy-start.14
  86.5 28.1 %exchange.2 = bf16[128,4,128]{2,1,0:T(4,128)(2,1)} custom-call(bf16[128,4,128]{2,1,0:T(4,128)(2,1)} %bitcast.40), custom_call_target="tpu_custom_call" | custom-call | tf_op jit(solution)/shard_map/exchange/pallas_call | solution.py:183
  114.6 0.0 copy-done.14
  114.6 1.0 pad_maximum_fusion
  115.6 0.0 copy-start.18
  115.6 0.2 copy.38
  115.9 0.6 copy-done.18
  116.5 0.0 copy-start.17
  116.5 0.3 fusion.20
  116.7 0.5 copy-done.17
  117.3 0.0 copy-start.19
  117.3 0.3 fusion
  117.6 0.5 copy-done.19
  118.1 0.0 copy-start.16
  118.1 0.3 fusion.19
  118.4 0.5 copy-done.16
  119.0 0.0 copy-start.5
  119.0 0.0 copy-start.6
  119.0 0.0 copy-start.7
  119.0 0.3 fusion.1
  119.3 0.6 copy-done.5
  119.9 0.1 copy-done.6
  119.9 0.0 copy-done.7
  119.9 0.0 copy-start.8
  119.9 1.0 fusion.11
  121.0 0.0 copy-done.8
  121.0 1.0 convolution_add_fusion
  122.0 1.0 fusion.12
  123.0 1.0 convolution_subtract_fusion
  124.0 0.1 multiply_add_fusion.1
  124.1 0.4 fusion.21
  124.5 0.4 convolution_add_fusion.3
  124.8 0.4 fusion.22
  125.2 0.0 copy-start.9
  125.2 0.0 copy-start.10
  125.2 0.0 copy-start.15
  125.3 0.4 convolution_subtract_fusion.1
  125.6 0.5 copy-done.9
  126.1 0.1 copy-done.10
  126.2 0.1 copy-done.15
  126.3 0.0 copy-start.11
  126.3 0.6 fusion.7
  126.9 0.3 copy-done.11
  127.2 0.6 fusion.3
  127.8 0.8 copy.57
  128.6 0.0 copy-start.12
  128.6 0.0 copy-start.13
  128.6 30.3 %exchange.3 = bf16[128,4,128]{2,1,0:T(4,128)(2,1)} custom-call(bf16[128,4,128]{2,1,0:T(4,128)(2,1)} %bitcast.42), custom_call_target="tpu_custom_call" | custom-call | tf_op jit(solution)/shard_map/exchange/pallas_call | solution.py:183
  158.9 0.0 copy-done.12
  158.9 0.0 copy-done.13
  158.9 1.7 %fusion.14 = (bf16[512,128]{1,0:T(8,128)(2,1)}, bf16[512,128]{1,0:T(8,128)(2,1)}) fusion(bf16[512,128]{1,0:T(8,128)(2,1)} %bitcast.41, bf16[512,128]{1,0:T(8,128)(2,1)S(1)} %copy-done.12, bf16[512,128]{1,0:T(8,128)(2,1)S(1)} %copy-done.13), kind=kLoop, calls=%fused_computation.27 | loop fusion | flops 458752 | bytes 655360 | tf_op jit(solution)/shard_map/convert_element_type | solution.py:246
  160.5 0.7 copy.59
Async XLA Ops:
  0.6 0.9 copy-start
  1.5 0.9 copy-start.1
  2.4 0.9 copy-start.2
  3.3 0.8 copy-start.4
  85.8 0.7 copy-start.3
  86.5 28.1 %copy-start.14 = (bf16[4,16384]{1,0:T(4,128)(2,1)S(1)}, bf16[4,16384]{1,0:T(4,128)(2,1)}, u32[]{:S(2)}) copy-start(bf16[4,16384]{1,0:T(4,128)(2,1)} %param.27) | copy-start | bytes 393220
  115.6 0.8 copy-start.18
  116.5 0.8 copy-start.17
  117.3 0.8 copy-start.19
  118.1 0.8 copy-start.16
  119.0 0.9 copy-start.5
  119.0 1.0 copy-start.6
  119.0 1.0 copy-start.7
  119.9 1.0 copy-start.8
  125.2 0.9 copy-start.9
  125.2 1.0 copy-start.10
  125.2 1.0 copy-start.15
  126.3 0.9 copy-start.11
  128.6 30.3 %copy-start.12 = (bf16[512,128]{1,0:T(8,128)(2,1)S(1)}, bf16[512,128]{1,0:T(8,128)(2,1)}, u32[]{:S(2)}) copy-start(bf16[512,128]{1,0:T(8,128)(2,1)} %param.25) | copy-start | bytes 393220
  128.6 30.3 %copy-start.13 = (bf16[512,128]{1,0:T(8,128)(2,1)S(1)}, bf16[512,128]{1,0:T(8,128)(2,1)}, u32[]{:S(2)}) copy-start(bf16[512,128]{1,0:T(8,128)(2,1)} %param.26) | copy-start | bytes 393220

commit v2 on v1

v2 whole, which is shorter than its diff:
```python
import jax
import jax.numpy as jnp
import ml_dtypes
import numpy as np
from jax import lax
from jax.experimental import pallas as pl
from jax.experimental.pallas import tpu as pltpu
from jax.sharding import PartitionSpec as P

MESH = pl.DeviceIdType.MESH
VMEM = pltpu.VMEM
F32 = jnp.float32
BF16 = jnp.bfloat16
ZN = 32
CHAN = 8
SEQ = 128
CH = 4
ROWS = 144
WIDTH = SEQ * CH


def seq_index(x, z, core):
    return (x * ZN + z) * 2 + core


def split(values):
    high = values.astype(BF16)
    return high, (values - high.astype(F32)).astype(BF16)


def dot(a, b):
    return jnp.dot(a, b, preferred_element_type=F32)


def wide_dot(values, high, low):
    a, b = split(values)
    return dot(a, high) + (dot(b, high) + dot(a, low))


def dot_wide(high, low, values):
    a, b = split(values)
    return dot(high, a) + (dot(high, b) + dot(low, a))


def kernel(g_hbm, w_hbm, gate_hbm, conv_hbm, key_hbm, value_hbm, filt_hbm,
           t1h_hbm, t1l_hbm, twc_hbm, tws_hbm, t2h_hbm, t2l_hbm, t4h_hbm, t4l_hbm,
           gg_ref, gk_ref, gv_ref,
           wf, gf, acc, gate, conv, key, value, filt,
           t1h, t1l, twc, tws, t2h, t2l, t4h, t4l,
           perm, back, turned, spec, out1, in1, out2, in2,
           recv_r, recv_l, recv_x, recv_p, recv_q, recv_gx, recv_gy, send_w, send_q, send_g,
           recv_1, sent_1, recv_2, sent_2, local, loads):
    me = lax.axis_index("seq")
    chan = lax.axis_index("chan")
    x, z, core = me // (2 * ZN), lax.rem(me // 2, ZN), lax.rem(me, 2)
    zr, zl = lax.rem(z + 1, ZN), lax.rem(z + ZN - 1, ZN)
    right, left = seq_index(x, zr, core), seq_index(x, zl, core)
    partner, across = seq_index(x, z, 1 - core), seq_index(1 - x, z, core)
    y, x_hi = chan // 2, lax.rem(chan, 2)
    opposite = y * 2 + 1 - x_hi
    rows = [lax.rem(y + step, 4) * 2 + x_hi for step in (1, 3, 2)]

    barrier = pltpu.get_barrier_semaphore()
    for peer in (right, left, partner, across):
        pl.semaphore_signal(barrier, inc=1, device_id={"seq": peer}, device_id_type=MESH)
    for peer in (opposite, *rows):
        pl.semaphore_signal(barrier, inc=1, device_id={"chan": peer}, device_id_type=MESH)
    own_w = pltpu.make_async_copy(w_hbm, wf.at[x, z, core], local.at[0])
    own_g = pltpu.make_async_copy(g_hbm, gf.at[chan], local.at[1])
    own_w.start()
    own_g.start()
    early = [(filt_hbm, filt), (t1h_hbm, t1h), (t1l_hbm, t1l), (twc_hbm, twc), (tws_hbm, tws), (t2h_hbm, t2h), (t2l_hbm, t2l)]
    late = [(gate_hbm, gate), (conv_hbm, conv), (key_hbm, key), (value_hbm, value), (t4h_hbm, t4h), (t4l_hbm, t4l)]
    pulls = [pltpu.make_async_copy(src, dst, loads.at[n]) for n, (src, dst) in enumerate(early + late)]
    for pull in pulls:
        pull.start()
    pl.semaphore_wait(barrier, 8)

    def send(src, slot_z, target, recv_sem):
        pltpu.make_async_remote_copy(
            src_ref=src, dst_ref=wf.at[x, slot_z, core], send_sem=send_w, recv_sem=recv_sem,
            device_id={"seq": target}, device_id_type=MESH,
        ).start()

    def send_g_to(src, slot, target, recv_sem):
        pltpu.make_async_remote_copy(
            src_ref=src, dst_ref=gf.at[slot], send_sem=send_g, recv_sem=recv_sem,
            device_id={"chan": target}, device_id_type=MESH,
        ).start()

    send(w_hbm, z, right, recv_r.at[0])
    send(w_hbm, z, left, recv_l.at[0])
    send(w_hbm, z, across, recv_x)
    send(w_hbm, z, partner, recv_p)
    send_g_to(g_hbm, chan, opposite, recv_gx)
    for peer in rows:
        send_g_to(g_hbm, chan, peer, recv_gy)

    def arrived(here, sem):
        pltpu.make_async_copy(here, here, sem).wait()

    def outer_inner(blocks):
        beside = jnp.concatenate([blocks[c * SEQ:(c + 1) * SEQ] for c in range(CH)], axis=1)
        part = dot(t1h[...], beside) + dot(t1l[...], beside)
        for c in range(CH):
            re, im = part[:ROWS, c * SEQ:(c + 1) * SEQ], part[ROWS:, c * SEQ:(c + 1) * SEQ]
            turned[c * ROWS:(c + 1) * ROWS, :SEQ] = re * twc[...] - im * tws[...]
            turned[c * ROWS:(c + 1) * ROWS, SEQ:] = re * tws[...] + im * twc[...]

    def hop(k, _):
        from_left, from_right = lax.rem(z + 2 * ZN - 1 - k, ZN), lax.rem(z + 1 + k, ZN)
        shard, other = wf.at[x, from_left, core], wf.at[x, from_right, core]
        arrived(shard, recv_r.at[k])
        send(shard, from_left, right, recv_r.at[k + 1])
        arrived(other, recv_l.at[k])

        @pl.when(k < 14)
        def _():
            send(other, from_right, left, recv_l.at[k + 1])

        send(shard, from_left, across, recv_x)
        send(other, from_right, across, recv_x)
        send(shard, from_left, partner, recv_p)
        send(other, from_right, partner, recv_p)

        @pl.when(k == 3)
        def _():
            arrived(gf.at[opposite], recv_gx)
            for peer in rows:
                send_g_to(gf.at[opposite], opposite, peer, recv_gy)

        @pl.when(k == 4)
        def _():
            row = lax.broadcasted_iota(jnp.int32, (WIDTH, WIDTH), 0)
            col = lax.broadcasted_iota(jnp.int32, (WIDTH, WIDTH), 1)
            perm[...] = jnp.where(col == (row % SEQ) * CH + row // SEQ, 1.0, 0.0).astype(BF16)
            for pull in pulls[:len(early)]:
                pull.wait()

        @pl.when(k == 5)
        def _():
            row = lax.broadcasted_iota(jnp.int32, (WIDTH, WIDTH), 0)
            col = lax.broadcasted_iota(jnp.int32, (WIDTH, WIDTH), 1)
            back[...] = jnp.where(col == (row % CH) * SEQ + row // CH, 1.0, 0.0).astype(BF16)

        @pl.when(k == 6)
        def _():
            outer_inner(dot(perm[...], filt.reshape(WIDTH, SEQ)[...]).astype(BF16))

        @pl.when(k == 8)
        def _():
            spec[...] = wide_dot(turned[...], t2h[...], t2l[...])

        return 0

    lax.fori_loop(0, 15, hop, 0)
    last = lax.rem(z + 16, ZN)
    shard = wf.at[x, last, core]
    arrived(shard, recv_r.at[15])
    send(shard, last, across, recv_x)
    send(shard, last, partner, recv_p)

    quarter = wf.at[1 - x, :, core]
    arrived(quarter, recv_x)
    pltpu.make_async_remote_copy(
        src_ref=quarter, dst_ref=quarter, send_sem=send_q, recv_sem=recv_q,
        device_id={"seq": partner}, device_id_type=MESH,
    ).start()

    own_w.wait()
    own_g.wait()
    for pull in pulls[len(early):]:
        pull.wait()
    arrived(gf.at[pl.ds(0, 6)], recv_gy)
    arrived(wf.at[x, :, 1 - core], recv_p)
    arrived(wf.at[1 - x, :, 1 - core], recv_q)

    acc[...] = jnp.zeros_like(acc)

    def multiply(j, _):
        block = wf[j // 4, pl.ds(lax.rem(j, 4) * 8, 8)].reshape(512, 512)
        acc[...] += dot(gf[j], block)
        return 0

    lax.fori_loop(0, CHAN, multiply, 0)
    mix = acc[...].T
    out1.reshape(WIDTH, SEQ)[...] = (mix * gate[...].astype(F32)).astype(BF16)
    gg_ref[...] = (mix * conv[...].astype(F32)).astype(BF16)

    def exchange(src, dst, recv, sent):
        own = pltpu.make_async_copy(src.at[me], dst.at[me], local.at[2])
        own.start()

        def body(m, _):
            away = 16 - (m + 1) // 2
            there = lax.rem(z + ZN + away * (2 * lax.rem(m, 2) - 1), ZN)

            def go(flip_x, flip_core):
                peer = seq_index(x + flip_x * (1 - 2 * x), there, core + flip_core * (1 - 2 * core))
                pltpu.make_async_remote_copy(
                    src_ref=src.at[peer], dst_ref=dst.at[me], send_sem=sent, recv_sem=recv,
                    device_id={"seq": peer}, device_id_type=MESH,
                ).start()

            go(1, 0)
            go(1, 1)
            go(0, 1)

            @pl.when(m < ZN - 1)
            def _():
                go(0, 0)

            return 0

        lax.fori_loop(0, ZN, body, 0)
        own.wait()
        most = dst.at[pl.ds(0, SEQ - 1)]
        arrived(most, recv)
        return lambda: arrived(most, sent)

    finish_1 = exchange(out1, in1, recv_1, sent_1)

    outer_inner(dot(perm[...], in1.reshape(WIDTH, SEQ)[...]).astype(BF16))
    ours = wide_dot(turned[...], t2h[...], t2l[...])
    a_re, a_im = ours[:, :SEQ], ours[:, SEQ:]
    k_re, k_im = spec[:, :SEQ], spec[:, SEQ:]
    joined = jnp.concatenate([k_re * a_re + k_im * a_im, k_im * a_re - k_re * a_im], axis=1)
    deep = wide_dot(joined, t2h[...], t2l[...])
    parts = []
    for c in range(CH):
        re, im = deep[c * ROWS:(c + 1) * ROWS, :SEQ], deep[c * ROWS:(c + 1) * ROWS, SEQ:]
        parts.append(jnp.concatenate([re * twc[...] - im * tws[...], -(im * twc[...] + re * tws[...])], axis=0))
    full = dot_wide(t4h[...], t4l[...], jnp.concatenate(parts, axis=1)).astype(BF16)
    stacked = jnp.concatenate([full[:, c * SEQ:(c + 1) * SEQ] for c in range(CH)], axis=0)
    out2.reshape(WIDTH, SEQ)[...] = dot(back[...], stacked).astype(BF16)

    finish_2 = exchange(out2, in2, recv_2, sent_2)
    inner = in2.reshape(WIDTH, SEQ)[...].astype(F32)
    gk_ref[...] = (inner * value[...].astype(F32)).astype(BF16)
    gv_ref[...] = (inner * key[...].astype(F32)).astype(BF16)

    finish_1()
    finish_2()
    arrived(quarter, send_q)
    arrived(gf.at[pl.ds(0, 7)], send_g)
    for amount in (quarter, quarter, wf.at[x, pl.ds(0, 31), core]):
        arrived(amount, send_w)


def tables():
    total = 2 * SEQ * SEQ
    kept = np.arange(ROWS)
    used = kept <= SEQ
    block, tau = np.arange(SEQ), np.arange(SEQ)
    outer = 2 * np.pi * (np.outer(kept, block) % (2 * SEQ)) / (2 * SEQ)
    cos, sin = np.cos(outer) * used[:, None], -np.sin(outer) * used[:, None]
    twist = 2 * np.pi * np.outer(kept, tau) / total
    inner = 2 * np.pi * (np.outer(tau, tau) % SEQ) / SEQ
    c, s = np.cos(inner), -np.sin(inner)
    weight = np.where((kept == 0) | (kept == SEQ), 1.0, 2.0)[:, None] / total
    first = np.concatenate([cos, sin], axis=0)
    second = np.block([[c, s], [-s, c]])
    fourth = np.concatenate([cos * weight, sin * weight], axis=0).T

    def pair(v):
        v = v.astype(np.float32)
        high = v.astype(ml_dtypes.bfloat16)
        return high, (v - high.astype(np.float32)).astype(ml_dtypes.bfloat16)

    return (*pair(first), np.cos(twist).astype(np.float32), (-np.sin(twist)).astype(np.float32), *pair(second), *pair(fourth))


def per_device(grad_out, out_weight, gate_stream, conv_output, key_stream, value_stream, long_filter):
    filters = jnp.swapaxes(long_filter.reshape(CH, SEQ, SEQ), 0, 1)
    consts = [jnp.asarray(t) for t in tables()]
    space, anywhere = pl.BlockSpec(memory_space=VMEM), pl.BlockSpec(memory_space=pl.ANY)
    dma = pltpu.SemaphoreType.DMA
    stream = jax.ShapeDtypeStruct((WIDTH, SEQ), BF16)
    streams = [VMEM((WIDTH, SEQ), BF16)] * 4
    blocks = VMEM((SEQ, CH, SEQ), BF16)
    return pl.pallas_call(
        kernel,
        out_shape=(stream, stream, stream),
        in_specs=[anywhere] * 15,
        out_specs=(space, space, space),
        scratch_shapes=[
            VMEM((2, ZN, 2, 32, 512), BF16), VMEM((CHAN, SEQ, 512), BF16), VMEM((SEQ, 512), F32),
            *streams, blocks,
            *[VMEM(t.shape, t.dtype) for t in consts],
            VMEM((WIDTH, WIDTH), BF16), VMEM((WIDTH, WIDTH), BF16),
            VMEM((CH * ROWS, 2 * SEQ), F32), VMEM((CH * ROWS, 2 * SEQ), F32),
            blocks, blocks, blocks, blocks,
            dma((16,)), dma((16,)), dma, dma, dma, dma, dma, dma, dma, dma,
            dma, dma, dma, dma, dma((3,)), dma((13,)),
        ],
        compiler_params=pltpu.CompilerParams(collective_id=0, has_side_effects=True, vmem_limit_bytes=48 << 20),
        name="hyena_backward",
    )(grad_out, out_weight, gate_stream, conv_output, key_stream, value_stream, filters, *consts)


def solution(mesh):
    in_specs = (
        P("seq", "chan"), P("seq", "chan"), P("chan", "seq"), P("chan", "seq"),
        P("chan", "seq"), P("chan", "seq"), P(("chan", "seq"), None),
    )
    out_specs = (P("chan", "seq"), P("chan", "seq"), P("chan", "seq"))
    return jax.shard_map(per_device, mesh=mesh, in_specs=in_specs, out_specs=out_specs, check_vma=False)
```

time: 162 us -> 129 us (0.80)
  Pallas kernels: 140 us -> 113 us
  matrix products: 7.84 us -> 0 us
  local copies, waits for them, and re-layouts: 9.63 us -> 15.3 us
  other arithmetic: 2.83 us -> 0 us
    pallas_call x3 -> x1, Pallas kernels: 140 us -> 113 us  [per_device(): pl.pallas_call(kernel, out_shape=(stream, stream, stream), in_specs=[anyw...]
    dot_general x14 -> x0, matrix products: 7.84 us -> none  [the longest x10 6.69 us: wide(): jnp.einsum(spec, a, b, precision=lax.Precision.HIGH, preferred_element_ty...]
    unnamed x42 -> x33, local copies, waits for them, and re-layouts: 9.41 us -> 15.3 us
    convert_element_type x1 -> x0, other arithmetic: 1.67 us -> none  [per_device(): (grad_inner * key_stream.astype(jnp.float32)).astype(jnp.bfloat16)]
where the time goes in v2:
time: 129 us
  Pallas kernels  113 us (88%)
  local copies, waits for them, and re-layouts  15.3 us (12%)
    pallas_call x1, Pallas kernels, per_device(): pl.pallas_call(kernel, out_shape=(stream, stream, stream), in_specs=[anyw...  113 us
    unnamed x33, local copies, waits for them, and re-layouts  15.3 us

profile of v2, /device:TPU:1, one launch (start us, length us, event | category | flops | bytes accessed | tf_op | source)
XLA Modules:
  0.0 128.8 jit_solution(934832630572834752)
XLA Ops:
  0.6 0.0 copy-start
  0.6 0.9 copy-done
  1.5 0.0 copy-start.1
  1.5 0.9 copy-done.1
  2.4 0.0 copy-start.2
  2.4 0.9 copy-done.2
  3.3 0.0 copy-start.3
  3.3 0.9 copy-done.3
  4.3 0.0 copy-start.4
  4.3 0.9 copy-done.4
  5.2 0.0 copy-start.5
  5.2 0.9 copy-done.5
  6.1 0.0 copy-start.6
  6.1 0.9 copy-done.6
  7.0 0.0 copy-start.7
  7.0 0.9 copy-done.7
  7.9 0.0 copy-start.8
  7.9 0.9 copy-done.8
  8.8 0.0 copy-start.9
  8.8 0.9 copy-done.9
  9.7 0.0 copy-start.10
  9.7 0.9 copy-done.10
  10.5 0.0 copy-start.11
  10.5 0.9 copy-done.11
  11.4 0.0 copy-start.12
  11.4 0.9 copy-done.12
  12.3 0.0 copy-start.13
  12.3 0.9 copy-done.13
  13.2 0.0 copy-start.14
  13.2 0.8 copy-done.14
  14.0 112.9 %hyena_backward.1 = (bf16[512,128]{1,0:T(8,128)(2,1)S(1)}, bf16[512,128]{1,0:T(8,128)(2,1)S(1)}, bf16[512,128]{1,0:T(8,128)(2,1)S(1)}) custom-call(bf16[128,512]{1,0:T(8,128)(2,1)S(1)} %copy-done, bf16[32,512]{1,0:T(8,128)(2,1)S(1)} %copy-done.14, bf16[512,128]{1,0:T(8,128)(2,1)S(1)} %copy-done.1, bf16[512,128]{1,0:T(8,128)(2,1)S(1)} %copy-done.2, ...), custom_call_target="tpu_custom_call" | custom-call | tf_op jit(solution)/shard_map/hyena_backward/pallas_call | solution.py:281
  126.8 0.7 copy.21
  127.5 0.7 copy.22
  128.1 0.7 copy.23
Async XLA Ops:
  0.6 0.9 copy-start
  1.5 0.9 copy-start.1
  2.4 0.9 copy-start.2
  3.3 0.9 copy-start.3
  4.3 0.9 copy-start.4
  5.2 0.9 copy-start.5
  6.1 0.9 copy-start.6
  7.0 0.9 copy-start.7
  7.9 0.9 copy-start.8
  8.8 0.9 copy-start.9
  9.7 0.9 copy-start.10
  10.5 0.9 copy-start.11
  11.4 0.9 copy-start.12
  12.3 0.9 copy-start.13
  13.2 0.8 copy-start.14

commit v3 on v2

--- a/solution.py
+++ b/solution.py
@@ -16,6 +16,9 @@
 SEQ = 128
 CH = 4
 ROWS = 144
+JUMP = 3
+GROUPS = 5
+LAG = 3
 WIDTH = SEQ * CH
 
 
@@ -53,15 +56,16 @@
     me = lax.axis_index("seq")
     chan = lax.axis_index("chan")
     x, z, core = me // (2 * ZN), lax.rem(me // 2, ZN), lax.rem(me, 2)
-    zr, zl = lax.rem(z + 1, ZN), lax.rem(z + ZN - 1, ZN)
-    right, left = seq_index(x, zr, core), seq_index(x, zl, core)
+    def along(step):
+        return seq_index(x, lax.rem(z + ZN + step, ZN), core)
+
     partner, across = seq_index(x, z, 1 - core), seq_index(1 - x, z, core)
     y, x_hi = chan // 2, lax.rem(chan, 2)
     opposite = y * 2 + 1 - x_hi
     rows = [lax.rem(y + step, 4) * 2 + x_hi for step in (1, 3, 2)]
 
     barrier = pltpu.get_barrier_semaphore()
-    for peer in (right, left, partner, across):
+    for peer in (along(1), along(-1), along(JUMP), along(-JUMP), partner, across):
         pl.semaphore_signal(barrier, inc=1, device_id={"seq": peer}, device_id_type=MESH)
     for peer in (opposite, *rows):
         pl.semaphore_signal(barrier, inc=1, device_id={"chan": peer}, device_id_type=MESH)
@@ -74,11 +78,11 @@
     pulls = [pltpu.make_async_copy(src, dst, loads.at[n]) for n, (src, dst) in enumerate(early + late)]
     for pull in pulls:
         pull.start()
-    pl.semaphore_wait(barrier, 8)
-
-    def send(src, slot_z, target, recv_sem):
+    pl.semaphore_wait(barrier, 10)
+
+    def send(src, slot_x, slot_z, target, send_sem, recv_sem):
         pltpu.make_async_remote_copy(
-            src_ref=src, dst_ref=wf.at[x, slot_z, core], send_sem=send_w, recv_sem=recv_sem,
+            src_ref=src, dst_ref=wf.at[slot_x, slot_z, core], send_sem=send_sem, recv_sem=recv_sem,
             device_id={"seq": target}, device_id_type=MESH,
         ).start()
 
@@ -88,10 +92,11 @@
             device_id={"chan": target}, device_id_type=MESH,
         ).start()
 
-    send(w_hbm, z, right, recv_r.at[0])
-    send(w_hbm, z, left, recv_l.at[0])
-    send(w_hbm, z, across, recv_x)
-    send(w_hbm, z, partner, recv_p)
+    for step in (JUMP, 1):
+        send(w_hbm, x, z, along(step), send_w, recv_r.at[step])
+        send(w_hbm, x, z, along(-step), send_w, recv_l.at[step])
+    send(w_hbm, x, z, across, send_w, recv_x.at[GROUPS])
+    send(w_hbm, x, z, partner, send_w, recv_p)
     send_g_to(g_hbm, chan, opposite, recv_gx)
     for peer in rows:
         send_g_to(g_hbm, chan, peer, recv_gy)
@@ -107,65 +112,96 @@
             turned[c * ROWS:(c + 1) * ROWS, :SEQ] = re * twc[...] - im * tws[...]
             turned[c * ROWS:(c + 1) * ROWS, SEQ:] = re * tws[...] + im * twc[...]
 
-    def hop(k, _):
-        from_left, from_right = lax.rem(z + 2 * ZN - 1 - k, ZN), lax.rem(z + 1 + k, ZN)
-        shard, other = wf.at[x, from_left, core], wf.at[x, from_right, core]
-        arrived(shard, recv_r.at[k])
-        send(shard, from_left, right, recv_r.at[k + 1])
-        arrived(other, recv_l.at[k])
-
-        @pl.when(k < 14)
-        def _():
-            send(other, from_right, left, recv_l.at[k + 1])
-
-        send(shard, from_left, across, recv_x)
-        send(other, from_right, across, recv_x)
-        send(shard, from_left, partner, recv_p)
-        send(other, from_right, partner, recv_p)
-
-        @pl.when(k == 3)
+    def slot(sign, away):
+        return lax.rem(z + 2 * ZN - sign * away, ZN)
+
+    def land(sign, away):
+        arrived(wf.at[x, slot(sign, away), core], (recv_r if sign > 0 else recv_l).at[away])
+
+    def relay(sign, away, step):
+        source = slot(sign, away)
+        send(wf.at[x, source, core], x, source, along(sign * step), send_w, (recv_r if sign > 0 else recv_l).at[away + step])
+
+    def spread(sign, away, group):
+        source = slot(sign, away)
+        shard = wf.at[x, source, core]
+        send(shard, x, source, across, send_w, recv_x.at[group])
+        send(shard, x, source, partner, send_w, recv_p)
+
+    def hand_over(sign, away):
+        source = slot(sign, away)
+        send(wf.at[1 - x, source, core], 1 - x, source, partner, send_q, recv_q)
+
+    def hand_over_group(group):
+        arrived(wf.at[1 - x, pl.ds(0, 2 * JUMP), core], recv_x.at[group])
+        for away in range(1, JUMP + 1):
+            hand_over(1, JUMP * group + away)
+            hand_over(-1, JUMP * group + away)
+
+    def prepare(group):
+        @pl.when(group == 0)
         def _():
             arrived(gf.at[opposite], recv_gx)
             for peer in rows:
                 send_g_to(gf.at[opposite], opposite, peer, recv_gy)
 
-        @pl.when(k == 4)
+        @pl.when(group == 1)
         def _():
             row = lax.broadcasted_iota(jnp.int32, (WIDTH, WIDTH), 0)
             col = lax.broadcasted_iota(jnp.int32, (WIDTH, WIDTH), 1)
-            perm[...] = jnp.where(col == (row % SEQ) * CH + row // SEQ, 1.0, 0.0).astype(BF16)
+            perm[...] = jnp.where(col == ((row & (SEQ - 1)) << 2 | row >> 7), 1.0, 0.0).astype(BF16)
+            back[...] = jnp.where(col == ((row & (CH - 1)) << 7 | row >> 2), 1.0, 0.0).astype(BF16)
             for pull in pulls[:len(early)]:
                 pull.wait()
 
-        @pl.when(k == 5)
-        def _():
-            row = lax.broadcasted_iota(jnp.int32, (WIDTH, WIDTH), 0)
-            col = lax.broadcasted_iota(jnp.int32, (WIDTH, WIDTH), 1)
-            back[...] = jnp.where(col == (row % CH) * SEQ + row // CH, 1.0, 0.0).astype(BF16)
-
-        @pl.when(k == 6)
+        @pl.when(group == 2)
         def _():
             outer_inner(dot(perm[...], filt.reshape(WIDTH, SEQ)[...]).astype(BF16))
 
-        @pl.when(k == 8)
+        @pl.when(group == 3)
         def _():
             spec[...] = wide_dot(turned[...], t2h[...], t2l[...])
 
+    def advance(group, _):
+        near, middle, far = JUMP * group + 1, JUMP * group + 2, JUMP * group + 3
+        for sign in (1, -1):
+            land(sign, near)
+            relay(sign, near, 1)
+        for sign in (1, -1):
+            land(sign, far)
+
+            @pl.when(group < GROUPS - 1)
+            def _():
+                relay(sign, far, JUMP)
+                relay(sign, far, 1)
+
+        for sign in (1, -1):
+            spread(sign, near, group)
+            spread(sign, far, group)
+
+        @pl.when(group == GROUPS - 1)
+        def _():
+            relay(1, far, 1)
+
+        prepare(group)
+        for sign in (1, -1):
+            land(sign, middle)
+            spread(sign, middle, group)
+
+        @pl.when(group >= LAG)
+        def _():
+            hand_over_group(group - LAG)
+
         return 0
 
-    lax.fori_loop(0, 15, hop, 0)
-    last = lax.rem(z + 16, ZN)
-    shard = wf.at[x, last, core]
-    arrived(shard, recv_r.at[15])
-    send(shard, last, across, recv_x)
-    send(shard, last, partner, recv_p)
-
+    lax.fori_loop(0, GROUPS, advance, 0)
+    land(1, 16)
+    spread(1, 16, GROUPS)
+    lax.fori_loop(GROUPS - LAG, GROUPS, lambda group, _: (hand_over_group(group), 0)[1], 0)
+    arrived(wf.at[1 - x, pl.ds(0, 2), core], recv_x.at[GROUPS])
+    hand_over(1, 0)
+    hand_over(1, 16)
     quarter = wf.at[1 - x, :, core]
-    arrived(quarter, recv_x)
-    pltpu.make_async_remote_copy(
-        src_ref=quarter, dst_ref=quarter, send_sem=send_q, recv_sem=recv_q,
-        device_id={"seq": partner}, device_id_type=MESH,
-    ).start()
 
     own_w.wait()
     own_g.wait()
@@ -273,7 +309,7 @@
 def per_device(grad_out, out_weight, gate_stream, conv_output, key_stream, value_stream, long_filter):
     filters = jnp.swapaxes(long_filter.reshape(CH, SEQ, SEQ), 0, 1)
     consts = [jnp.asarray(t) for t in tables()]
-    space, anywhere = pl.BlockSpec(memory_space=VMEM), pl.BlockSpec(memory_space=pl.ANY)
+    space, anywhere = pl.BlockSpec(memory_space=VMEM), pl.BlockSpec(memory_space=pltpu.HBM)
     dma = pltpu.SemaphoreType.DMA
     stream = jax.ShapeDtypeStruct((WIDTH, SEQ), BF16)
     streams = [VMEM((WIDTH, SEQ), BF16)] * 4
@@ -290,10 +326,10 @@
             VMEM((WIDTH, WIDTH), BF16), VMEM((WIDTH, WIDTH), BF16),
             VMEM((CH * ROWS, 2 * SEQ), F32), VMEM((CH * ROWS, 2 * SEQ), F32),
             blocks, blocks, blocks, blocks,
-            dma((16,)), dma((16,)), dma, dma, dma, dma, dma, dma, dma, dma,
+            dma((17,)), dma((16,)), dma((GROUPS + 1,)), dma, dma, dma, dma, dma, dma, dma,
             dma, dma, dma, dma, dma((3,)), dma((13,)),
         ],
-        compiler_params=pltpu.CompilerParams(collective_id=0, has_side_effects=True, vmem_limit_bytes=48 << 20),
+        compiler_params=pltpu.CompilerParams(collective_id=0, has_side_effects=True),
         name="hyena_backward",
     )(grad_out, out_weight, gate_stream, conv_output, key_stream, value_stream, filters, *consts)
 

time: 129 us -> 96.8 us (0.75)
  Pallas kernels: 113 us -> 92.7 us
  local copies, waits for them, and re-layouts: 15.3 us -> 3.21 us
    pallas_call x1, Pallas kernels: 113 us -> 92.7 us  [per_device(): pl.pallas_call(kernel, out_shape=(stream, stream, stream), in_specs=[anyw...]
    unnamed x33 -> x7, local copies, waits for them, and re-layouts: 15.3 us -> 3.21 us
where the time goes in v3:
time: 96.8 us; the launch traced here: 96.6 us
  Pallas kernels  92.7 us (96%)
  local copies, waits for them, and re-layouts  3.21 us (3%)
    pallas_call x1, Pallas kernels, per_device(): pl.pallas_call(kernel, out_shape=(stream, stream, stream), in_specs=[anyw...  92.7 us
    unnamed x7, local copies, waits for them, and re-layouts  3.21 us

profile of v3, /device:TPU:1, one launch (start us, length us, event | category | flops | bytes accessed | tf_op | source)
XLA Modules:
  0.0 96.6 jit_solution(11302759398135019361)
XLA Ops:
  0.6 92.7 %hyena_backward.1 = (bf16[512,128]{1,0:T(8,128)(2,1)}, bf16[512,128]{1,0:T(8,128)(2,1)}, bf16[512,128]{1,0:T(8,128)(2,1)}) custom-call(bf16[128,512]{1,0:T(8,128)(2,1)} %g_hbm.1, bf16[32,512]{1,0:T(8,128)(2,1)} %w_hbm.1, bf16[512,128]{1,0:T(8,128)(2,1)} %gate_hbm.1, bf16[512,128]{1,0:T(8,128)(2,1)} %conv_hbm.1, bf16[512,128]{1,0:T(8,128)(2,1)} %key_hbm.1, ...), custom_call_target="tpu_custom_call" | custom-call | tf_op jit(solution)/shard_map/hyena_backward/pallas_call | solution.py:317
  93.4 0.0 copy-start.1
  93.4 1.6 %copy.21 = bf16[512,128]{1,0:T(8,128)(2,1)} copy(bf16[512,128]{1,0:T(8,128)(2,1)} %get-tuple-element.6) | data formatting | bytes 262144
  95.0 0.0 copy-done.1
  95.0 0.0 copy-start
  95.0 0.7 copy.22
  95.6 0.3 copy-done
  95.9 0.7 copy.23
Async XLA Ops:
  93.4 1.6 %copy-start.1 = (bf16[512,128]{1,0:T(8,128)(2,1)S(1)}, bf16[512,128]{1,0:T(8,128)(2,1)}, u32[]{:S(2)}) copy-start(bf16[512,128]{1,0:T(8,128)(2,1)} %get-tuple-element.7) | copy-start | bytes 393220
  95.0 1.0 copy-start

commit v4 on v3

--- a/solution.py
+++ b/solution.py
@@ -47,7 +47,7 @@
 
 def kernel(g_hbm, w_hbm, gate_hbm, conv_hbm, key_hbm, value_hbm, filt_hbm,
            t1h_hbm, t1l_hbm, twc_hbm, tws_hbm, t2h_hbm, t2l_hbm, t4h_hbm, t4l_hbm,
-           gg_ref, gk_ref, gv_ref,
+           grads,
            wf, gf, acc, gate, conv, key, value, filt,
            t1h, t1l, twc, tws, t2h, t2l, t4h, t4l,
            perm, back, turned, spec, out1, in1, out2, in2,
@@ -197,31 +197,34 @@
     lax.fori_loop(0, GROUPS, advance, 0)
     land(1, 16)
     spread(1, 16, GROUPS)
-    lax.fori_loop(GROUPS - LAG, GROUPS, lambda group, _: (hand_over_group(group), 0)[1], 0)
+    lax.fori_loop(GROUPS - LAG, GROUPS - 1, lambda group, _: (hand_over_group(group), 0)[1], 0)
+    own_w.wait()
+    own_g.wait()
+    for pull in pulls[len(early):]:
+        pull.wait()
+    acc[...] = jnp.zeros_like(acc)
+    arrived(gf.at[pl.ds(0, 6)], recv_gy)
+
+    def multiply(side):
+        def body(j, _):
+            block = wf[side, pl.ds(j * 8, 8)].reshape(512, 512)
+            acc[...] += dot(gf[side * 4 + j], block)
+            return 0
+
+        lax.fori_loop(0, 4, body, 0)
+
+    arrived(wf.at[x, :, 1 - core], recv_p)
+    multiply(x)
+    hand_over_group(GROUPS - 1)
     arrived(wf.at[1 - x, pl.ds(0, 2), core], recv_x.at[GROUPS])
     hand_over(1, 0)
     hand_over(1, 16)
     quarter = wf.at[1 - x, :, core]
-
-    own_w.wait()
-    own_g.wait()
-    for pull in pulls[len(early):]:
-        pull.wait()
-    arrived(gf.at[pl.ds(0, 6)], recv_gy)
-    arrived(wf.at[x, :, 1 - core], recv_p)
     arrived(wf.at[1 - x, :, 1 - core], recv_q)
-
-    acc[...] = jnp.zeros_like(acc)
-
-    def multiply(j, _):
-        block = wf[j // 4, pl.ds(lax.rem(j, 4) * 8, 8)].reshape(512, 512)
-        acc[...] += dot(gf[j], block)
-        return 0
-
-    lax.fori_loop(0, CHAN, multiply, 0)
+    multiply(1 - x)
     mix = acc[...].T
     out1.reshape(WIDTH, SEQ)[...] = (mix * gate[...].astype(F32)).astype(BF16)
-    gg_ref[...] = (mix * conv[...].astype(F32)).astype(BF16)
+    grads[0] = (mix * conv[...].astype(F32)).astype(BF16)
 
     def exchange(src, dst, recv, sent):
         own = pltpu.make_async_copy(src.at[me], dst.at[me], local.at[2])
@@ -272,8 +275,8 @@
 
     finish_2 = exchange(out2, in2, recv_2, sent_2)
     inner = in2.reshape(WIDTH, SEQ)[...].astype(F32)
-    gk_ref[...] = (inner * value[...].astype(F32)).astype(BF16)
-    gv_ref[...] = (inner * key[...].astype(F32)).astype(BF16)
+    grads[1] = (inner * value[...].astype(F32)).astype(BF16)
+    grads[2] = (inner * key[...].astype(F32)).astype(BF16)
 
     finish_1()
     finish_2()
@@ -311,14 +314,13 @@
     consts = [jnp.asarray(t) for t in tables()]
     space, anywhere = pl.BlockSpec(memory_space=VMEM), pl.BlockSpec(memory_space=pltpu.HBM)
     dma = pltpu.SemaphoreType.DMA
-    stream = jax.ShapeDtypeStruct((WIDTH, SEQ), BF16)
     streams = [VMEM((WIDTH, SEQ), BF16)] * 4
     blocks = VMEM((SEQ, CH, SEQ), BF16)
-    return pl.pallas_call(
+    grads = pl.pallas_call(
         kernel,
-        out_shape=(stream, stream, stream),
+        out_shape=jax.ShapeDtypeStruct((3, WIDTH, SEQ), BF16),
         in_specs=[anywhere] * 15,
-        out_specs=(space, space, space),
+        out_specs=space,
         scratch_shapes=[
             VMEM((2, ZN, 2, 32, 512), BF16), VMEM((CHAN, SEQ, 512), BF16), VMEM((SEQ, 512), F32),
             *streams, blocks,
@@ -332,6 +334,7 @@
         compiler_params=pltpu.CompilerParams(collective_id=0, has_side_effects=True),
         name="hyena_backward",
     )(grad_out, out_weight, gate_stream, conv_output, key_stream, value_stream, filters, *consts)
+    return (grads[0], grads[1], grads[2])
 
 
 def solution(mesh):

time: 96.8 us -> 95.4 us (0.986)
  local copies, waits for them, and re-layouts: 3.21 us -> 1.78 us
    unnamed x7 -> x0, local copies, waits for them, and re-layouts: 3.21 us -> none
    squeeze x0 -> x1, local copies, waits for them, and re-layouts: none -> 1.78 us  [per_device(): return (grads[0], grads[1], grads[2])]
where the time goes in v4:
time: 95.4 us; the launch traced here: 95.2 us
  Pallas kernels  92.8 us (97%)
  local copies, waits for them, and re-layouts  1.78 us (2%)
    pallas_call x1, Pallas kernels, per_device(): pl.pallas_call(kernel, out_shape=jax.ShapeDtypeStruct((3, WIDTH, SEQ), BF...  92.8 us

profile of v4, /device:TPU:1, one launch (start us, length us, event | category | flops | bytes accessed | tf_op | source)
XLA Modules:
  0.0 95.2 jit_solution(4098507310730267318)
XLA Ops:
  0.6 92.8 %hyena_backward.1 = bf16[3,512,128]{2,1,0:T(8,128)(2,1)} custom-call(bf16[128,512]{1,0:T(8,128)(2,1)} %g_hbm.1, bf16[32,512]{1,0:T(8,128)(2,1)} %w_hbm.1, bf16[512,128]{1,0:T(8,128)(2,1)} %gate_hbm.1, bf16[512,128]{1,0:T(8,128)(2,1)} %conv_hbm.1, bf16[512,128]{1,0:T(8,128)(2,1)} %key_hbm.1, bf16[512,128]{1,0:T(8,128)(2,1)} %value_hbm.1, ...), custom_call_target="tpu_custom_call" | custom-call | tf_op jit(solution)/shard_map/hyena_backward/pallas_call | solution.py:319
  93.4 1.8 %slice_bitcast_fusion = (bf16[512,128]{1,0:T(8,128)(2,1)}, bf16[512,128]{1,0:T(8,128)(2,1)}, bf16[512,128]{1,0:T(8,128)(2,1)}) fusion(bf16[3,512,128]{2,1,0:T(8,128)(2,1)} %hyena_backward.1), kind=kLoop, calls=%fused_computation | loop fusion | bytes 786432 | tf_op jit(solution)/shard_map/squeeze | solution.py:337
